TPU v7x, 32 devices: a whole 2x2x4 slice. The times are simulated.
32 devices in a mesh: gx: 4 (over y, x), gy: 8 (over z, core).
Axes of the slice: x: 2, y: 2, z: 4, core: 2. Of those that a mesh axis runs over, the one named last changes fastest.
Arguments:
- schur_blocks: float32 [32, 2048, 2048], P(('gx', 'gy')), may hold values from -1 to 11, as said below
- offsets: int32 [32], P(('gx', 'gy')), may hold values from 256 to 768, as said below
- right_side: float32 [32768, 128], P(('gx', 'gy')), may hold values from -20 to 20
- coarse_basis: float32 [32768, 128], P(('gx', 'gy')), may hold values from -0.03125 to 0.03125
- coarse_load: float32 [128, 128], replicated, may hold values from -6 to 6
Outputs:
- multipliers: float32 [32768, 128], P(('gx', 'gy'))
- amplitudes: float32 [128, 128], replicated
Inputs may be any that keep to these rules, and one draw needn't show every extreme that they name: `schur_blocks`: each block is symmetric positive definite. `offsets`: both ends of the range are taken by some subdomain.
All inputs are finite; a program needn't handle non-finite values.
Results may differ from a plain program's by a relative error of at most 0.0003.
Values sent between devices are 32-bit elements; how exact they have to be, the bound alone decides.
A program may use at most 128 MiB of HBM per device.

v0:
```python
import jax
import jax.numpy as jnp
from jax import lax
from jax.sharding import PartitionSpec as P

ITERS = 3
HIGHEST = lax.Precision.HIGHEST


def extended_2(block, sides, width):
    for axis, dim in sides:
        count = lax.axis_size(axis)
        forward = [(i, i + 1) for i in range(count - 1)]
        backward = [(target, source) for source, target in forward]
        low = lax.ppermute(
            lax.slice_in_dim(block, block.shape[dim] - width, None, axis=dim), axis, forward
        )
        high = lax.ppermute(lax.slice_in_dim(block, 0, width, axis=dim), axis, backward)
        block = jnp.concatenate([low, block, high], axis=dim)
    return block


def from_behind(value, axis, steps):
    count = lax.axis_size(axis)
    initial, last = (max(0, -steps), min(count, count - steps))
    return lax.ppermute(value, axis, [(source, source + steps) for source in range(initial, last)])


def apply_local(vector, schur_block, start_row):
    slab_rows = vector.shape[0]
    window_rows = schur_block.shape[0]
    extended = extended_2(vector, ((("gx", "gy"), 0),), slab_rows)
    window = lax.dynamic_slice_in_dim(extended, start_row, window_rows, 0)
    product_block = jnp.dot(
        schur_block, window, precision=HIGHEST, preferred_element_type=jnp.float32
    )
    spread = jnp.zeros((3 * slab_rows, vector.shape[1]), jnp.float32)
    spread = lax.dynamic_update_slice_in_dim(spread, product_block, start_row, 0)
    to_left = spread[:slab_rows]
    own_part = spread[slab_rows : 2 * slab_rows]
    to_right = spread[2 * slab_rows :]
    from_right = from_behind(to_left, ("gx", "gy"), -1)
    from_left = from_behind(to_right, ("gx", "gy"), 1)
    result = own_part + from_left + from_right
    return result


def project_sum(residual, coarse_basis, gram_factor):
    local_coarse = jnp.dot(
        coarse_basis.T, residual, precision=HIGHEST, preferred_element_type=jnp.float32
    )
    coarse_part, squares = lax.psum(
        (local_coarse, jnp.sum(residual * residual, axis=0)), ("gx", "gy")
    )
    amplitudes = jax.scipy.linalg.cho_solve((gram_factor, True), coarse_part)
    projected = residual - jnp.dot(
        coarse_basis, amplitudes, precision=HIGHEST, preferred_element_type=jnp.float32
    )
    energy = squares - jnp.sum(amplitudes * coarse_part, axis=0)
    return (projected, amplitudes, energy)


def local(schur_blocks, offsets, right_side, coarse_basis, coarse_load):
    schur_block = schur_blocks[0]
    start_row = offsets[0]
    local_gram = jnp.dot(
        coarse_basis.T, coarse_basis, precision=HIGHEST, preferred_element_type=jnp.float32
    )
    gram_matrix = lax.psum(local_gram, ("gx", "gy"))
    gram_factor = jnp.linalg.cholesky(gram_matrix)
    start_load = jax.scipy.linalg.cho_solve((gram_factor, True), coarse_load)
    multipliers = jnp.dot(
        coarse_basis, start_load, precision=HIGHEST, preferred_element_type=jnp.float32
    )
    residual = right_side - apply_local(multipliers, schur_block, start_row)
    projected, amplitudes, energy_now = project_sum(residual, coarse_basis, gram_factor)
    direction = projected
    for iteration in range(ITERS):
        operator_image = apply_local(direction, schur_block, start_row)
        curvature = lax.psum(jnp.sum(direction * operator_image, axis=0), ("gx", "gy"))
        step_length = energy_now / curvature
        multipliers = multipliers + step_length * direction
        residual = residual - step_length * operator_image
        projected, amplitudes, energy_next = project_sum(residual, coarse_basis, gram_factor)
        direction = projected + energy_next / energy_now * direction
        energy_now = energy_next
    return (multipliers, amplitudes)


def solution(mesh):
    in_specs = (
        P(("gx", "gy"), None, None),
        P(("gx", "gy")),
        P(("gx", "gy"), None),
        P(("gx", "gy"), None),
        P(),
    )
    out_specs = (P(("gx", "gy"), None), P())
    return jax.shard_map(local, mesh=mesh, in_specs=in_specs, out_specs=out_specs, check_vma=False)
```

profile of v0, /device:TPU:1, one launch (start us, length us, event | category | flops | bytes accessed | tf_op | source)
XLA Modules:
  0.0 1052.4 jit_solution(16787756393830020999)
XLA Ops:
  9.9 127.6 %all-reduce.7.cloned.1.call-done = f32[128,128]{0,1:T(8,128)} async-done(((f32[128,128]{0,1:T(8,128)}), f32[128,128]{0,1:T(8,128)}) %all-reduce.7.cloned.1.call-update) | async-done | bytes 65552 | tf_op jit(solution)/shard_map/psum | solution.py:69
  139.3 11.7 %cholesky.18 = f32[128,128]{1,0:T(8,128)S(1)} custom-call(f32[128,128]{1,0:T(8,128)S(1)} %fusion.66), custom_call_target="Cholesky" | custom-call | tf_op jit(solution)/shard_map/jit(cholesky)/cholesky | solution.py:70
  152.3 9.8 custom-call.12
  172.6 7.9 collective-permute-done.1
  180.5 20.9 %fusion.8 = f32[2048,128]{0,1:T(8,128)} fusion(f32[1,2048,2048]{2,1,0:T(8,128)} %param.7, s32[]{:T(128)S(6)} %select_n.7, f32[1024,128]{0,1:T(8,128)S(1)} %collective-permute-done, f32[1024,128]{0,1:T(8,128)S(1)} %convolution_bitcast_fusion.3, f32[1024,128]{0,1:T(8,128)S(1)} %collective-permute-done.1), kind=kOutput, calls=%fused_computation.8 | convolution fusion | flops 6442975232 | bytes 19398660 | tf_op jit(solution)/shard_map/dot_general | solution.py:34
  201.6 5.3 dynamic_update_slice.12
  209.9 3.6 collective-permute-start.2
  213.7 5.0 collective-permute-done.3
  222.7 128.0 %all-reduce.9.cloned.1.call-done = f32[128,128]{0,1:T(8,128)} async-done(((f32[128,128]{0,1:T(8,128)}), f32[128,128]{0,1:T(8,128)}) %all-reduce.9.cloned.1.call-update) | async-done | bytes 65552 | tf_op jit(solution)/shard_map/psum | solution.py:52
  357.8 4.2 collective-permute-done.4
  362.0 7.9 collective-permute-done.5
  369.9 20.9 %fusion.11 = f32[2048,128]{0,1:T(8,128)} fusion(f32[1,2048,2048]{2,1,0:T(8,128)} %param.7, s32[]{:T(128)S(6)} %select_n.7, f32[1024,128]{0,1:T(8,128)S(1)} %collective-permute-done.4, f32[1024,128]{0,1:T(8,128)S(1)} %fusion.20, f32[1024,128]{0,1:T(8,128)S(1)} %collective-permute-done.5), kind=kOutput, calls=%fused_computation.9 | convolution fusion | flops 6442975232 | bytes 19398660 | tf_op jit(solution)/shard_map/dot_general | solution.py:34
  390.9 5.3 dynamic_update_slice.13
  403.1 4.9 collective-permute-done.7
  410.5 44.6 %all-reduce = (f32[128]{0:T(128)S(1)}, f32[128]{0:T(128)S(1)}) all-reduce(f32[128]{0:T(128)S(1)} %get-tuple-element.17, f32[128]{0:T(128)S(1)} %multiply_reduce_fusion.4), channel_id=1, replica_groups=mesh['gx'=4,'gy'=8] {'gx','gy'}, use_global_device_ids=true, to_apply=%region_4.6 | all-reduce | flops 256 | bytes 2048 | tf_op jit(solution)/shard_map/psum | solution.py:52
  458.1 41.6 %psum.81 = f32[128]{0:T(128)S(1)} all-reduce(f32[128]{0:T(128)S(1)} %get-tuple-element.13), channel_id=1, replica_groups=mesh['gx'=4,'gy'=8] {'gx','gy'}, use_global_device_ids=true, to_apply=%region_10.12 | all-reduce | flops 128 | bytes 1024 | tf_op jit(solution)/shard_map/psum | solution.py:52
  499.7 81.1 %all-reduce.11.cloned.1.call-done = f32[128,128]{0,1:T(8,128)} async-done(((f32[128,128]{0,1:T(8,128)}), f32[128,128]{0,1:T(8,128)}) %all-reduce.11.cloned.1.call-update) | async-done | bytes 65552 | tf_op jit(solution)/shard_map/psum | solution.py:52
  589.0 4.2 collective-permute-done.8
  593.2 7.9 collective-permute-done.9
  601.0 20.9 %fusion.14 = f32[2048,128]{0,1:T(8,128)} fusion(f32[1,2048,2048]{2,1,0:T(8,128)} %param.7, s32[]{:T(128)S(6)} %select_n.7, f32[1024,128]{0,1:T(8,128)S(1)} %collective-permute-done.8, f32[1024,128]{0,1:T(8,128)S(1)} %fusion.22, f32[1024,128]{0,1:T(8,128)S(1)} %collective-permute-done.9), kind=kOutput, calls=%fused_computation.10 | convolution fusion | flops 6442975232 | bytes 19398660 | tf_op jit(solution)/shard_map/dot_general | solution.py:34
  622.1 5.3 dynamic_update_slice.14
  633.1 4.9 collective-permute-done.11
  640.2 45.2 %psum.83 = f32[128]{0:T(128)S(1)} all-reduce(f32[128]{0:T(128)S(1)} %multiply_reduce_fusion.2), channel_id=1, replica_groups=mesh['gx'=4,'gy'=8] {'gx','gy'}, use_global_device_ids=true, to_apply=%region_14.16 | all-reduce | flops 128 | bytes 1024 | tf_op jit(solution)/shard_map/psum | solution.py:80
  690.0 40.7 %psum.84 = f32[128]{0:T(128)S(1)} all-reduce(f32[128]{0:T(128)S(1)} %get-tuple-element.9), channel_id=1, replica_groups=mesh['gx'=4,'gy'=8] {'gx','gy'}, use_global_device_ids=true, to_apply=%region_16.18 | all-reduce | flops 128 | bytes 1024 | tf_op jit(solution)/shard_map/psum | solution.py:52
  730.7 81.9 %all-reduce.13.cloned.1.call-done = f32[128,128]{0,1:T(8,128)} async-done(((f32[128,128]{0,1:T(8,128)}), f32[128,128]{0,1:T(8,128)}) %all-reduce.13.cloned.1.call-update) | async-done | bytes 65552 | tf_op jit(solution)/shard_map/psum | solution.py:52
  822.1 4.0 collective-permute-done.12
  826.0 7.9 collective-permute-done.13
  833.9 20.9 %fusion.17 = f32[2048,128]{0,1:T(8,128)} fusion(f32[1,2048,2048]{2,1,0:T(8,128)} %param.7, s32[]{:T(128)S(6)} %select_n.7, f32[1024,128]{0,1:T(8,128)S(1)} %collective-permute-done.12, f32[1024,128]{0,1:T(8,128)S(1)} %fusion.24, f32[1024,128]{0,1:T(8,128)S(1)} %collective-permute-done.13), kind=kOutput, calls=%fused_computation.11 | convolution fusion | flops 6442975232 | bytes 19398660 | tf_op jit(solution)/shard_map/dot_general | solution.py:34
  854.9 5.3 dynamic_update_slice.15
  866.1 4.9 collective-permute-done.15
  873.2 45.1 %psum.86 = f32[128]{0:T(128)S(1)} all-reduce(f32[128]{0:T(128)S(1)} %multiply_reduce_fusion), channel_id=1, replica_groups=mesh['gx'=4,'gy'=8] {'gx','gy'}, use_global_device_ids=true, to_apply=%region_20.22 | all-reduce | flops 128 | bytes 1024 | tf_op jit(solution)/shard_map/psum | solution.py:80
  923.5 120.2 %all-reduce.15.cloned.1.call-done = f32[128,128]{0,1:T(8,128)} async-done(((f32[128,128]{0,1:T(8,128)}), f32[128,128]{0,1:T(8,128)}) %all-reduce.15.cloned.1.call-update) | async-done | bytes 65552 | tf_op jit(solution)/shard_map/psum | solution.py:52
  (110 shorter events, 87.6 us)
Async XLA Ops:
  7.2 155.0 %copy-start.13 = (f32[128,128]{1,0:T(8,128)S(1)}, f32[128,128]{1,0:T(8,128)}, u32[]{:S(2)}) copy-start(f32[128,128]{1,0:T(8,128)} %param.11) | copy-start | bytes 196612
  7.2 130.3 %all-reduce.7.cloned.1.call-start = ((), (), s32[]{:S(2)}) async-start(), calls=%async_computation | async-start | bytes 131072 | tf_op jit(solution)/shard_map/psum | solution.py:69
  9.9 340.8 %all-reduce.9.cloned.1.call-start = ((), (), s32[]{:S(2)}) async-start(), calls=%async_computation.1 | async-start | bytes 131072 | tf_op jit(solution)/shard_map/psum | solution.py:52
  163.3 38.1 %copy-start.5 = (f32[1024,128]{0,1:T(8,128)}, f32[1024,128]{0,1:T(8,128)S(1)}, u32[]{:S(2)}) copy-start(f32[1024,128]{0,1:T(8,128)S(1)} %convolution_bitcast_fusion.3) | copy-start | bytes 1572868
  163.3 9.3 collective-permute-start
  166.5 14.0 %collective-permute-start.1 = (f32[1024,128]{0,1:T(8,128)S(1)}, f32[1024,128]{0,1:T(8,128)S(1)}, u32[]{:S(2)}, u32[]{:S(2)}) collective-permute-start(f32[1024,128]{0,1:T(8,128)S(1)} %convolution_bitcast_fusion.3), channel_id=1, source_target_pairs={{1,0},{2,1},{3,2},{4,3},{5,4},{6,5},{7,6},{8,7},{9,8},{10,9},{11,1... | collective-permute-start | bytes 1572872 | tf_op jit(solution)/shard_map/ppermute | solution.py:18
  206.9 6.6 copy-start.11
  207.9 10.8 %collective-permute-start.3 = (f32[1024,128]{0,1:T(8,128)}, f32[1024,128]{0,1:T(8,128)}, u32[]{:S(2)}, u32[]{:S(2)}) collective-permute-start(f32[1024,128]{0,1:T(8,128)} %get-tuple-element.26), channel_id=1, source_target_pairs={{1,0},{2,1},{3,2},{4,3},{5,4},{6,5},{7,6},{8,7},{9,8},{10,9},{11,1... | collective-permute-start | bytes 1572872 | tf_op jit(solution)/shard_map/ppermute | solution.py:26
  209.9 10.1 collective-permute-start.2
  221.3 131.4 %copy-start.4 = (f32[1024,128]{0,1:T(8,128)}, f32[1024,128]{0,1:T(8,128)S(1)}, u32[]{:S(2)}) copy-start(f32[1024,128]{0,1:T(8,128)S(1)} %get-tuple-element.18) | copy-start | bytes 1572868
  222.6 358.2 %all-reduce.11.cloned.1.call-start = ((), (), s32[]{:S(2)}) async-start(), calls=%async_computation.2 | async-start | bytes 131072 | tf_op jit(solution)/shard_map/psum | solution.py:52
  352.7 9.3 collective-permute-start.4
  355.9 14.0 %collective-permute-start.5 = (f32[1024,128]{0,1:T(8,128)S(1)}, f32[1024,128]{0,1:T(8,128)S(1)}, u32[]{:S(2)}, u32[]{:S(2)}) collective-permute-start(f32[1024,128]{0,1:T(8,128)S(1)} %fusion.20), channel_id=1, source_target_pairs={{1,0},{2,1},{3,2},{4,3},{5,4},{6,5},{7,6},{8,7},{9,8},{10,9},{11,1... | collective-permute-start | bytes 1572872 | tf_op jit(solution)/shard_map/ppermute | solution.py:18
  396.3 6.7 copy-start.12
  397.3 10.7 %collective-permute-start.7 = (f32[1024,128]{0,1:T(8,128)}, f32[1024,128]{0,1:T(8,128)S(1)}, u32[]{:S(2)}, u32[]{:S(2)}) collective-permute-start(f32[1024,128]{0,1:T(8,128)} %get-tuple-element.24), channel_id=1, source_target_pairs={{1,0},{2,1},{3,2},{4,3},{5,4},{6,5},{7,6},{8,7},{9,8},{10,9},{11,1... | collective-permute-start | bytes 1572872 | tf_op jit(solution)/shard_map/ppermute | solution.py:26
  399.2 10.1 collective-permute-start.6
  408.0 47.1 %copy-start.6 = (f32[1024,128]{0,1:T(8,128)}, f32[1024,128]{0,1:T(8,128)S(1)}, u32[]{:S(2)}) copy-start(f32[1024,128]{0,1:T(8,128)S(1)} %collective-permute-done.7) | copy-start | bytes 1572868
  456.8 127.1 %copy-start.1 = (f32[1024,128]{0,1:T(8,128)}, f32[1024,128]{0,1:T(8,128)S(1)}, u32[]{:S(2)}) copy-start(f32[1024,128]{0,1:T(8,128)S(1)} %get-tuple-element.14) | copy-start | bytes 1572868
  458.1 354.5 %all-reduce.13.cloned.1.call-start = ((), (), s32[]{:S(2)}) async-start(), calls=%async_computation.3 | async-start | bytes 131072 | tf_op jit(solution)/shard_map/psum | solution.py:52
  583.9 9.3 collective-permute-start.8
  587.1 14.0 %collective-permute-start.9 = (f32[1024,128]{0,1:T(8,128)S(1)}, f32[1024,128]{0,1:T(8,128)S(1)}, u32[]{:S(2)}, u32[]{:S(2)}) collective-permute-start(f32[1024,128]{0,1:T(8,128)S(1)} %fusion.22), channel_id=1, source_target_pairs={{1,0},{2,1},{3,2},{4,3},{5,4},{6,5},{7,6},{8,7},{9,8},{10,9},{11,1... | collective-permute-start | bytes 1572872 | tf_op jit(solution)/shard_map/ppermute | solution.py:18
  627.5 10.5 collective-permute-start.11
  629.4 9.8 collective-permute-start.10
  638.0 1.2 copy-start.7
  690.0 353.7 %all-reduce.15.cloned.1.call-start = ((), (), s32[]{:S(2)}) async-start(), calls=%async_computation.4 | async-start | bytes 131072 | tf_op jit(solution)/shard_map/psum | solution.py:52
  816.7 38.1 %copy-start.2 = (f32[1024,128]{0,1:T(8,128)}, f32[1024,128]{0,1:T(8,128)S(1)}, u32[]{:S(2)}) copy-start(f32[1024,128]{0,1:T(8,128)S(1)} %fusion.24) | copy-start | bytes 1572868
  816.7 9.3 collective-permute-start.12
  819.9 14.0 %collective-permute-start.13 = (f32[1024,128]{0,1:T(8,128)S(1)}, f32[1024,128]{0,1:T(8,128)S(1)}, u32[]{:S(2)}, u32[]{:S(2)}) collective-permute-start(f32[1024,128]{0,1:T(8,128)S(1)} %fusion.24), channel_id=1, source_target_pairs={{1,0},{2,1},{3,2},{4,3},{5,4},{6,5},{7,6},{8,7},{9,8},{10,9},{11,1... | collective-permute-start | bytes 1572872 | tf_op jit(solution)/shard_map/ppermute | solution.py:18
  860.3 12.7 %copy-start.3 = (f32[1024,128]{0,1:T(8,128)S(1)}, f32[1024,128]{0,1:T(8,128)}, u32[]{:S(2)}) copy-start(f32[1024,128]{0,1:T(8,128)} %copy-done.2) | copy-start | bytes 1572868
  860.4 10.6 %collective-permute-start.15 = (f32[1024,128]{0,1:T(8,128)S(1)}, f32[1024,128]{0,1:T(8,128)S(1)}, u32[]{:S(2)}, u32[]{:S(2)}) collective-permute-start(f32[1024,128]{0,1:T(8,128)S(1)} %get-tuple-element.20), channel_id=1, source_target_pairs={{1,0},{2,1},{3,2},{4,3},{5,4},{6,5},{7,6},{8,7},{9,8},{10,9},{11,1... | collective-permute-start | bytes 1572872 | tf_op jit(solution)/shard_map/ppermute | solution.py:26
  862.4 9.8 collective-permute-start.14
  871.0 1.2 copy-start.9
  (3 other events, 2.7 us)
Sparse Core Ops, SparseCore 0:
  14.1 123.3 all-reduce.6
  222.7 127.9 all-reduce.8
  458.2 122.5 all-reduce.10
  690.1 122.4 all-reduce.12
  921.2 122.4 all-reduce.14
where the time goes:
time: 1060 us; the launch traced here: 1050 us
  waiting for transfers between devices  610 us (58%)
  blocking collectives  217 us (20%)
  matrix products  103 us (10%)
  starting transfers between devices  43.7 us (4%)
  other arithmetic  34 us (3%)
  local copies, waits for them, and re-layouts  29.1 us (3%)
  between operations  15.2 us (1%)
    psum x4, waiting for transfers between devices, project_sum(): lax.psum((local_coarse, jnp.sum(residual * residual, axis=0)), ('gx', 'gy'))  411 us
    psum x1, waiting for transfers between devices, local(): gram_matrix = lax.psum(local_gram, ('gx', 'gy'))  128 us
    psum x3, blocking collectives, project_sum(): lax.psum((local_coarse, jnp.sum(residual * residual, axis=0)), ('gx', 'gy'))  127 us
    psum x2, blocking collectives, local(): lax.psum(jnp.sum(direction * operator_image, axis=0), ('gx', 'gy'))  90.3 us
    dot_general x4, matrix products, apply_local(): jnp.dot(schur_block, window, precision=HIGHEST, preferred_element_type=jn...  83.5 us
    ppermute x4, waiting for transfers between devices, extended_2(): lax.ppermute(lax.slice_in_dim(block, 0, width, axis=dim), axis, backward)  31.5 us
    ppermute x8, waiting for transfers between devices, from_behind(): lax.ppermute(value, axis, [(source, source + steps) for source in range(i...  24.6 us
    ppermute x8, starting transfers between devices, from_behind(): lax.ppermute(value, axis, [(source, source + steps) for source in range(i...  22.4 us
  transfers between devices with their start and end apart: 21, of which 21 were waited for; matrix products, arithmetic and copies ran while one was open for 0% of the time, Pallas kernels for 0%

commit v1 on v0

--- a/solution.py
+++ b/solution.py
@@ -66,7 +66,7 @@
     local_gram = jnp.dot(
         coarse_basis.T, coarse_basis, precision=HIGHEST, preferred_element_type=jnp.float32
     )
-    gram_matrix = lax.psum(local_gram, ("gx", "gy"))
+    gram_matrix = jnp.sum(lax.all_gather(local_gram, ("gx", "gy")), axis=0)
     gram_factor = jnp.linalg.cholesky(gram_matrix)
     start_load = jax.scipy.linalg.cho_solve((gram_factor, True), coarse_load)
     multipliers = jnp.dot(

time: 1060 us -> 994 us (0.938)
  waiting for transfers between devices: 610 us -> 545 us
    psum x1 -> x0, waiting for transfers between devices: 128 us -> none  [local(): gram_matrix = lax.psum(local_gram, ('gx', 'gy'))]
    all_gather x0 -> x1, waiting for transfers between devices: none -> 60.5 us  [local(): gram_matrix = jnp.sum(lax.all_gather(local_gram, ('gx', 'gy')), axis=0)]
where the time goes in v1:
time: 994 us; the launch traced here: 986 us
  waiting for transfers between devices  545 us (55%)
  blocking collectives  217 us (22%)
  matrix products  103 us (10%)
  starting transfers between devices  42.9 us (4%)
  other arithmetic  34.8 us (4%)
  local copies, waits for them, and re-layouts  28.3 us (3%)
  between operations  15.2 us (2%)
    psum x4, waiting for transfers between devices, project_sum(): lax.psum((local_coarse, jnp.sum(residual * residual, axis=0)), ('gx', 'gy'))  411 us
    psum x3, blocking collectives, project_sum(): lax.psum((local_coarse, jnp.sum(residual * residual, axis=0)), ('gx', 'gy'))  127 us
    psum x2, blocking collectives, local(): lax.psum(jnp.sum(direction * operator_image, axis=0), ('gx', 'gy'))  90.3 us
    dot_general x4, matrix products, apply_local(): jnp.dot(schur_block, window, precision=HIGHEST, preferred_element_type=jn...  83.5 us
    all_gather x1, waiting for transfers between devices, local(): gram_matrix = jnp.sum(lax.all_gather(local_gram, ('gx', 'gy')), axis=0)  60.5 us
    ppermute x4, waiting for transfers between devices, extended_2(): lax.ppermute(lax.slice_in_dim(block, 0, width, axis=dim), axis, backward)  33.6 us
    ppermute x8, waiting for transfers between devices, from_behind(): lax.ppermute(value, axis, [(source, source + steps) for source in range(i...  24.6 us
    ppermute x8, starting transfers between devices, from_behind(): lax.ppermute(value, axis, [(source, source + steps) for source in range(i...  22.4 us
  transfers between devices with their start and end apart: 21, of which 21 were waited for; matrix products, arithmetic and copies ran while one was open for 0% of the time, Pallas kernels for 0%

profile of v1, /device:TPU:1, one launch (start us, length us, event | category | flops | bytes accessed | tf_op | source)
XLA Modules:
  0.0 986.0 jit_solution(7353457414029650562)
XLA Ops:
  9.9 60.5 %all-gather.3.cloned.1.call-done = f32[4096,128]{1,0:T(8,128)} async-done(((f32[128,128]{1,0:T(8,128)}), f32[4096,128]{1,0:T(8,128)}) %all-gather.3.cloned.1.call-update) | async-done | bytes 2097168 | tf_op jit(solution)/shard_map/all_gather | solution.py:69
  72.2 11.7 %cholesky.18 = f32[128,128]{1,0:T(8,128)S(1)} custom-call(f32[128,128]{1,0:T(8,128)S(1)} %fusion.66), custom_call_target="Cholesky" | custom-call | tf_op jit(solution)/shard_map/jit(cholesky)/cholesky | solution.py:70
  85.3 9.8 custom-call.12
  104.7 9.9 %collective-permute-done.1 = f32[1024,128]{0,1:T(8,128)S(1)} collective-permute-done((f32[1024,128]{0,1:T(8,128)S(1)}, f32[1024,128]{0,1:T(8,128)S(1)}, u32[]{:S(2)}, u32[]{:S(2)}) %collective-permute-start.1) | collective-permute-done | bytes 524320 | tf_op jit(solution)/shard_map/ppermute | solution.py:18
  114.6 20.9 %fusion.8 = f32[2048,128]{0,1:T(8,128)} fusion(f32[1,2048,2048]{2,1,0:T(8,128)} %param.7, s32[]{:T(128)S(6)} %select_n.7, f32[1024,128]{0,1:T(8,128)S(1)} %collective-permute-done, f32[1024,128]{0,1:T(8,128)S(1)} %convolution_bitcast_fusion.3, f32[1024,128]{0,1:T(8,128)S(1)} %collective-permute-done.1), kind=kOutput, calls=%fused_computation.8 | convolution fusion | flops 6442975232 | bytes 19398660 | tf_op jit(solution)/shard_map/dot_general | solution.py:34
  135.7 5.3 dynamic_update_slice.12
  144.0 3.6 collective-permute-start.2
  147.8 5.0 collective-permute-done.3
  156.8 127.5 %all-reduce.6.cloned.1.call-done = f32[128,128]{0,1:T(8,128)} async-done(((f32[128,128]{0,1:T(8,128)}), f32[128,128]{0,1:T(8,128)}) %all-reduce.6.cloned.1.call-update) | async-done | bytes 65552 | tf_op jit(solution)/shard_map/psum | solution.py:52
  291.4 4.2 collective-permute-done.4
  295.6 7.9 collective-permute-done.5
  303.5 20.9 %fusion.11 = f32[2048,128]{0,1:T(8,128)} fusion(f32[1,2048,2048]{2,1,0:T(8,128)} %param.7, s32[]{:T(128)S(6)} %select_n.7, f32[1024,128]{0,1:T(8,128)S(1)} %collective-permute-done.4, f32[1024,128]{0,1:T(8,128)S(1)} %fusion.20, f32[1024,128]{0,1:T(8,128)S(1)} %collective-permute-done.5), kind=kOutput, calls=%fused_computation.9 | convolution fusion | flops 6442975232 | bytes 19398660 | tf_op jit(solution)/shard_map/dot_general | solution.py:34
  324.5 5.3 dynamic_update_slice.13
  336.7 4.9 collective-permute-done.7
  344.1 44.6 %all-reduce = (f32[128]{0:T(128)S(1)}, f32[128]{0:T(128)S(1)}) all-reduce(f32[128]{0:T(128)S(1)} %get-tuple-element.19, f32[128]{0:T(128)S(1)} %multiply_reduce_fusion.4), channel_id=1, replica_groups=mesh['gx'=4,'gy'=8] {'gx','gy'}, use_global_device_ids=true, to_apply=%region_4.6 | all-reduce | flops 256 | bytes 2048 | tf_op jit(solution)/shard_map/psum | solution.py:52
  391.7 41.6 %psum.73 = f32[128]{0:T(128)S(1)} all-reduce(f32[128]{0:T(128)S(1)} %get-tuple-element.15), channel_id=1, replica_groups=mesh['gx'=4,'gy'=8] {'gx','gy'}, use_global_device_ids=true, to_apply=%region_10.12 | all-reduce | flops 128 | bytes 1024 | tf_op jit(solution)/shard_map/psum | solution.py:52
  433.3 81.1 %all-reduce.8.cloned.1.call-done = f32[128,128]{0,1:T(8,128)} async-done(((f32[128,128]{0,1:T(8,128)}), f32[128,128]{0,1:T(8,128)}) %all-reduce.8.cloned.1.call-update) | async-done | bytes 65552 | tf_op jit(solution)/shard_map/psum | solution.py:52
  522.6 4.2 collective-permute-done.8
  526.8 7.9 collective-permute-done.9
  534.7 20.9 %fusion.14 = f32[2048,128]{0,1:T(8,128)} fusion(f32[1,2048,2048]{2,1,0:T(8,128)} %param.7, s32[]{:T(128)S(6)} %select_n.7, f32[1024,128]{0,1:T(8,128)S(1)} %collective-permute-done.8, f32[1024,128]{0,1:T(8,128)S(1)} %fusion.22, f32[1024,128]{0,1:T(8,128)S(1)} %collective-permute-done.9), kind=kOutput, calls=%fused_computation.10 | convolution fusion | flops 6442975232 | bytes 19398660 | tf_op jit(solution)/shard_map/dot_general | solution.py:34
  555.7 5.3 dynamic_update_slice.14
  566.7 4.9 collective-permute-done.11
  573.8 45.2 %psum.75 = f32[128]{0:T(128)S(1)} all-reduce(f32[128]{0:T(128)S(1)} %multiply_reduce_fusion.2), channel_id=1, replica_groups=mesh['gx'=4,'gy'=8] {'gx','gy'}, use_global_device_ids=true, to_apply=%region_14.16 | all-reduce | flops 128 | bytes 1024 | tf_op jit(solution)/shard_map/psum | solution.py:80
  623.6 40.7 %psum.76 = f32[128]{0:T(128)S(1)} all-reduce(f32[128]{0:T(128)S(1)} %get-tuple-element.11), channel_id=1, replica_groups=mesh['gx'=4,'gy'=8] {'gx','gy'}, use_global_device_ids=true, to_apply=%region_16.18 | all-reduce | flops 128 | bytes 1024 | tf_op jit(solution)/shard_map/psum | solution.py:52
  664.3 81.9 %all-reduce.10.cloned.1.call-done = f32[128,128]{0,1:T(8,128)} async-done(((f32[128,128]{0,1:T(8,128)}), f32[128,128]{0,1:T(8,128)}) %all-reduce.10.cloned.1.call-update) | async-done | bytes 65552 | tf_op jit(solution)/shard_map/psum | solution.py:52
  755.7 4.0 collective-permute-done.12
  759.7 7.9 collective-permute-done.13
  767.6 20.9 %fusion.17 = f32[2048,128]{0,1:T(8,128)} fusion(f32[1,2048,2048]{2,1,0:T(8,128)} %param.7, s32[]{:T(128)S(6)} %select_n.7, f32[1024,128]{0,1:T(8,128)S(1)} %collective-permute-done.12, f32[1024,128]{0,1:T(8,128)S(1)} %fusion.24, f32[1024,128]{0,1:T(8,128)S(1)} %collective-permute-done.13), kind=kOutput, calls=%fused_computation.11 | convolution fusion | flops 6442975232 | bytes 19398660 | tf_op jit(solution)/shard_map/dot_general | solution.py:34
  788.6 5.3 dynamic_update_slice.15
  799.7 4.9 collective-permute-done.15
  806.8 45.1 %psum.78 = f32[128]{0:T(128)S(1)} all-reduce(f32[128]{0:T(128)S(1)} %multiply_reduce_fusion), channel_id=1, replica_groups=mesh['gx'=4,'gy'=8] {'gx','gy'}, use_global_device_ids=true, to_apply=%region_20.22 | all-reduce | flops 128 | bytes 1024 | tf_op jit(solution)/shard_map/psum | solution.py:80
  857.1 120.2 %all-reduce.12.cloned.1.call-done = f32[128,128]{0,1:T(8,128)} async-done(((f32[128,128]{0,1:T(8,128)}), f32[128,128]{0,1:T(8,128)}) %all-reduce.12.cloned.1.call-update) | async-done | bytes 65552 | tf_op jit(solution)/shard_map/psum | solution.py:52
  (111 shorter events, 86.8 us)
Async XLA Ops:
  7.2 63.2 %all-gather.3.cloned.1.call-start = ((), (), s32[]{:S(2)}) async-start(), calls=%async_computation.4 | async-start | bytes 2162688 | tf_op jit(solution)/shard_map/all_gather | solution.py:69
  9.9 85.2 %copy-start.13 = (f32[128,128]{1,0:T(8,128)S(1)}, f32[128,128]{1,0:T(8,128)}, u32[]{:S(2)}) copy-start(f32[128,128]{1,0:T(8,128)} %param.11) | copy-start | bytes 196612
  9.9 274.4 %all-reduce.6.cloned.1.call-start = ((), (), s32[]{:S(2)}) async-start(), calls=%async_computation | async-start | bytes 131072 | tf_op jit(solution)/shard_map/psum | solution.py:52
  96.3 39.3 %copy-start.5 = (f32[1024,128]{0,1:T(8,128)}, f32[1024,128]{0,1:T(8,128)S(1)}, u32[]{:S(2)}) copy-start(f32[1024,128]{0,1:T(8,128)S(1)} %convolution_bitcast_fusion.3) | copy-start | bytes 1572868
  96.3 8.4 collective-permute-start
  98.6 16.0 %collective-permute-start.1 = (f32[1024,128]{0,1:T(8,128)S(1)}, f32[1024,128]{0,1:T(8,128)S(1)}, u32[]{:S(2)}, u32[]{:S(2)}) collective-permute-start(f32[1024,128]{0,1:T(8,128)S(1)} %convolution_bitcast_fusion.3), channel_id=1, source_target_pairs={{1,0},{2,1},{3,2},{4,3},{5,4},{6,5},{7,6},{8,7},{9,8},{10,9},{11,1... | collective-permute-start | bytes 1572872 | tf_op jit(solution)/shard_map/ppermute | solution.py:18
  141.0 6.6 copy-start.11
  142.1 10.8 %collective-permute-start.3 = (f32[1024,128]{0,1:T(8,128)}, f32[1024,128]{0,1:T(8,128)}, u32[]{:S(2)}, u32[]{:S(2)}) collective-permute-start(f32[1024,128]{0,1:T(8,128)} %get-tuple-element.28), channel_id=1, source_target_pairs={{1,0},{2,1},{3,2},{4,3},{5,4},{6,5},{7,6},{8,7},{9,8},{10,9},{11,1... | collective-permute-start | bytes 1572872 | tf_op jit(solution)/shard_map/ppermute | solution.py:26
  144.0 10.1 %collective-permute-start.2 = (f32[1024,128]{0,1:T(8,128)}, f32[1024,128]{0,1:T(8,128)}, u32[]{:S(2)}, u32[]{:S(2)}) collective-permute-start(f32[1024,128]{0,1:T(8,128)} %get-tuple-element.27), channel_id=1, source_target_pairs={{0,1},{1,2},{2,3},{3,4},{4,5},{5,6},{6,7},{7,8},{8,9},{9,10},{10,1... | collective-permute-start | bytes 1572872 | tf_op jit(solution)/shard_map/ppermute | solution.py:26
  155.4 130.9 %copy-start.4 = (f32[1024,128]{0,1:T(8,128)}, f32[1024,128]{0,1:T(8,128)S(1)}, u32[]{:S(2)}) copy-start(f32[1024,128]{0,1:T(8,128)S(1)} %get-tuple-element.20) | copy-start | bytes 1572868
  156.7 357.6 %all-reduce.8.cloned.1.call-start = ((), (), s32[]{:S(2)}) async-start(), calls=%async_computation.1 | async-start | bytes 131072 | tf_op jit(solution)/shard_map/psum | solution.py:52
  286.3 9.3 collective-permute-start.4
  289.5 14.0 %collective-permute-start.5 = (f32[1024,128]{0,1:T(8,128)S(1)}, f32[1024,128]{0,1:T(8,128)S(1)}, u32[]{:S(2)}, u32[]{:S(2)}) collective-permute-start(f32[1024,128]{0,1:T(8,128)S(1)} %fusion.20), channel_id=1, source_target_pairs={{1,0},{2,1},{3,2},{4,3},{5,4},{6,5},{7,6},{8,7},{9,8},{10,9},{11,1... | collective-permute-start | bytes 1572872 | tf_op jit(solution)/shard_map/ppermute | solution.py:18
  329.9 6.7 copy-start.12
  330.9 10.7 %collective-permute-start.7 = (f32[1024,128]{0,1:T(8,128)}, f32[1024,128]{0,1:T(8,128)S(1)}, u32[]{:S(2)}, u32[]{:S(2)}) collective-permute-start(f32[1024,128]{0,1:T(8,128)} %get-tuple-element.26), channel_id=1, source_target_pairs={{1,0},{2,1},{3,2},{4,3},{5,4},{6,5},{7,6},{8,7},{9,8},{10,9},{11,1... | collective-permute-start | bytes 1572872 | tf_op jit(solution)/shard_map/ppermute | solution.py:26
  332.8 10.1 %collective-permute-start.6 = (f32[1024,128]{0,1:T(8,128)}, f32[1024,128]{0,1:T(8,128)}, u32[]{:S(2)}, u32[]{:S(2)}) collective-permute-start(f32[1024,128]{0,1:T(8,128)} %get-tuple-element.25), channel_id=1, source_target_pairs={{0,1},{1,2},{2,3},{3,4},{4,5},{5,6},{6,7},{7,8},{8,9},{9,10},{10,1... | collective-permute-start | bytes 1572872 | tf_op jit(solution)/shard_map/ppermute | solution.py:26
  341.6 47.1 %copy-start.6 = (f32[1024,128]{0,1:T(8,128)}, f32[1024,128]{0,1:T(8,128)S(1)}, u32[]{:S(2)}) copy-start(f32[1024,128]{0,1:T(8,128)S(1)} %collective-permute-done.7) | copy-start | bytes 1572868
  390.4 127.1 %copy-start.1 = (f32[1024,128]{0,1:T(8,128)}, f32[1024,128]{0,1:T(8,128)S(1)}, u32[]{:S(2)}) copy-start(f32[1024,128]{0,1:T(8,128)S(1)} %get-tuple-element.16) | copy-start | bytes 1572868
  391.7 354.6 %all-reduce.10.cloned.1.call-start = ((), (), s32[]{:S(2)}) async-start(), calls=%async_computation.2 | async-start | bytes 131072 | tf_op jit(solution)/shard_map/psum | solution.py:52
  517.5 9.3 collective-permute-start.8
  520.7 14.0 %collective-permute-start.9 = (f32[1024,128]{0,1:T(8,128)S(1)}, f32[1024,128]{0,1:T(8,128)S(1)}, u32[]{:S(2)}, u32[]{:S(2)}) collective-permute-start(f32[1024,128]{0,1:T(8,128)S(1)} %fusion.22), channel_id=1, source_target_pairs={{1,0},{2,1},{3,2},{4,3},{5,4},{6,5},{7,6},{8,7},{9,8},{10,9},{11,1... | collective-permute-start | bytes 1572872 | tf_op jit(solution)/shard_map/ppermute | solution.py:18
  561.1 10.5 %collective-permute-start.11 = (f32[1024,128]{0,1:T(8,128)S(1)}, f32[1024,128]{0,1:T(8,128)S(1)}, u32[]{:S(2)}, u32[]{:S(2)}) collective-permute-start(f32[1024,128]{0,1:T(8,128)S(1)} %get-tuple-element.24), channel_id=1, source_target_pairs={{1,0},{2,1},{3,2},{4,3},{5,4},{6,5},{7,6},{8,7},{9,8},{10,9},{11,1... | collective-permute-start | bytes 1572872 | tf_op jit(solution)/shard_map/ppermute | solution.py:26
  563.0 9.8 collective-permute-start.10
  571.6 1.2 copy-start.7
  623.6 353.7 %all-reduce.12.cloned.1.call-start = ((), (), s32[]{:S(2)}) async-start(), calls=%async_computation.3 | async-start | bytes 131072 | tf_op jit(solution)/shard_map/psum | solution.py:52
  750.4 38.1 %copy-start.2 = (f32[1024,128]{0,1:T(8,128)}, f32[1024,128]{0,1:T(8,128)S(1)}, u32[]{:S(2)}) copy-start(f32[1024,128]{0,1:T(8,128)S(1)} %fusion.24) | copy-start | bytes 1572868
  750.4 9.3 collective-permute-start.12
  753.6 14.0 %collective-permute-start.13 = (f32[1024,128]{0,1:T(8,128)S(1)}, f32[1024,128]{0,1:T(8,128)S(1)}, u32[]{:S(2)}, u32[]{:S(2)}) collective-permute-start(f32[1024,128]{0,1:T(8,128)S(1)} %fusion.24), channel_id=1, source_target_pairs={{1,0},{2,1},{3,2},{4,3},{5,4},{6,5},{7,6},{8,7},{9,8},{10,9},{11,1... | collective-permute-start | bytes 1572872 | tf_op jit(solution)/shard_map/ppermute | solution.py:18
  793.9 12.7 %copy-start.3 = (f32[1024,128]{0,1:T(8,128)S(1)}, f32[1024,128]{0,1:T(8,128)}, u32[]{:S(2)}) copy-start(f32[1024,128]{0,1:T(8,128)} %copy-done.2) | copy-start | bytes 1572868
  794.0 10.6 %collective-permute-start.15 = (f32[1024,128]{0,1:T(8,128)S(1)}, f32[1024,128]{0,1:T(8,128)S(1)}, u32[]{:S(2)}, u32[]{:S(2)}) collective-permute-start(f32[1024,128]{0,1:T(8,128)S(1)} %get-tuple-element.22), channel_id=1, source_target_pairs={{1,0},{2,1},{3,2},{4,3},{5,4},{6,5},{7,6},{8,7},{9,8},{10,9},{11,1... | collective-permute-start | bytes 1572872 | tf_op jit(solution)/shard_map/ppermute | solution.py:26
  796.1 9.8 collective-permute-start.14
  804.6 1.2 copy-start.9
  (3 other events, 2.7 us)
Sparse Core Ops, SparseCore 0:
  11.5 58.8 all-gather.2
  156.9 127.4 all-reduce.5
  391.8 122.5 all-reduce.7
  623.7 122.4 all-reduce.9
  854.8 122.4 all-reduce.11
